TPU v7x, 512 devices: a whole 4x8x8 slice. The times are simulated.
512 devices in a mesh: row: 16 (over y, core), col: 32 (over x, z).
Axes of the slice: x: 4, y: 8, z: 8, core: 2. Of those that a mesh axis runs over, the one named last changes fastest.
Arguments:
- rhs: bfloat16 [4, 16, 32, 64, 256], P(None, 'row', 'col'), may hold values from -6 to 6
- dinv: float32 [4, 16, 32, 64, 64], P(None, 'row', 'col'), may hold values from -1.5 to 1.5, as said below
- lower: bfloat16 [6, 16, 32, 32, 64, 128], P(None, 'row', 'col'), may hold values from -0.0625 to 0.0625
- sources: int32 [6, 16, 32, 32, 2], P(None, 'row', 'col'), may hold values from -1 to 15, as said below
Outputs:
- solution: float32 [4, 16, 32, 64, 256], P(None, 'row', 'col')
Inputs may be any that keep to these rules, and one draw needn't show every extreme that they name: `dinv`: lower triangular. `sources`: for each level pair, holder and target, the live entries are distinct; in every level pair every device has a target with all 2 entries live.
All inputs are finite; a program needn't handle non-finite values.
Results may differ from a plain program's by a relative error of at most 0.002.
Values may be sent and summed in bfloat16 or wider, within the bound.
No kernel may reach another device: no remote copies, remote signals or barrier semaphores. Data moves between devices by JAX's collectives and lax.ppermute only.
A program may use at most 64 MiB of HBM per device.

v0:
```python
import jax
import jax.numpy as jnp
from jax import lax
from jax.sharding import PartitionSpec as P


def level_terms(blocks, indices, gathered):
    clipped = jnp.maximum(indices, 0)
    picked = jnp.take(gathered, clipped, axis=0)
    picked = jnp.where((indices >= 0)[:, :, None, None], picked, jnp.zeros((), gathered.dtype))
    peer_count, per_count, block_rows, rhs_width = picked.shape
    picked = picked.reshape(peer_count, per_count * block_rows, rhs_width)
    return jnp.einsum("qik,qkn->qin", blocks, picked, preferred_element_type=jnp.float32)


def on_device(rhs, dinv, lower, sources):
    levels = rhs.shape[0]
    pair_of = {}
    for section in range(levels):
        for target in range(section + 1, levels):
            pair_of[section, target] = len(pair_of)
    gathered = []
    results = []
    for section in range(levels):
        residual = rhs[section, 0, 0].astype(jnp.float32)
        if section:
            partial = None
            for earlier in range(section):
                pair = pair_of[earlier, section]
                term = level_terms(lower[pair, 0, 0], sources[pair, 0, 0], gathered[earlier])
                partial = term if partial is None else partial + term
            arrived = lax.all_to_all(
                partial.astype(jnp.bfloat16), "col", split_axis=0, concat_axis=0, tiled=True
            )
            residual = residual - jnp.sum(arrived.astype(jnp.float32), axis=0)
        solution = jnp.dot(
            dinv[section, 0, 0],
            residual,
            precision=lax.Precision.HIGHEST,
            preferred_element_type=jnp.float32,
        )
        results.append(solution)
        if section + 1 < levels:
            solved = solution.astype(jnp.bfloat16)
            gathered.append(lax.all_gather(solved[None], "row", axis=0, tiled=True))
    return jnp.stack(results)[:, None, None]


def solution(mesh):
    in_specs = (
        P(None, "row", "col", None, None),
        P(None, "row", "col", None, None),
        P(None, "row", "col", None, None, None),
        P(None, "row", "col", None, None),
    )
    out_specs = P(None, "row", "col", None, None)
    return jax.shard_map(
        on_device, mesh=mesh, in_specs=in_specs, out_specs=out_specs, check_vma=False
    )
```

profile of v0, /device:TPU:8, one launch (start us, length us, event | category | flops | bytes accessed | tf_op | source)
XLA Modules:
  0.0 183.5 jit_solution(16684669490472690284)
XLA Ops:
  0.0 1.3 compare_and_fusion.1
  1.3 1.4 compare_bitcast_fusion.1
  2.9 0.9 fusion.40
  3.8 21.4 %all-gather = bf16[1024,256]{1,0:T(8,128)(2,1)S(1)} all-gather(bf16[64,256]{1,0:T(8,128)(2,1)S(1)} %get-tuple-element.34), channel_id=2, replica_groups=mesh['row'=16,'col'=32] {'row'}, dimensions={0}, use_global_device_ids=true | all-gather | bytes 557056 | tf_op jit(solution)/shard_map/all_gather | solution.py:45
  25.4 0.7 gather_fusion
  26.5 2.5 %fusion = bf16[32,64,256]{2,1,0:T(8,128)(2,1)} fusion(bf16[32,128,256]{2,1,0:T(8,128)(2,1)S(1)} %bitcast.153, bf16[6,1,1,32,64,128]{5,4,3,2,1,0:T(8,128)(2,1)} %param.8), kind=kOutput, calls=%fused_computation.18 | convolution fusion | flops 134742016 | bytes 3670016 | tf_op jit(solution)/shard_map/qik,qkn->qin/dot_general | solution.py:13
  28.9 9.5 %all-to-all-start = ((bf16[32,64,256]{2,1,0:T(8,128)(2,1)}), bf16[32,64,256]{2,1,0:T(8,128)(2,1)}, u32[]{:S(2)}, u32[]{:S(2)}) async-start(bf16[32,64,256]{2,1,0:T(8,128)(2,1)} %fusion), calls=%async_computation | async-start | bytes 2097152 | tf_op jit(solution)/shard_map/all_to_all | solution.py:32
  39.1 0.7 gather_fusion.1
  40.3 2.9 %fusion.9 = f32[32,256,64]{1,2,0:T(8,128)} fusion(bf16[32,128,256]{2,1,0:T(8,128)(2,1)S(1)} %bitcast.159, bf16[6,1,1,32,64,128]{5,4,3,2,1,0:T(8,128)(2,1)} %param.8), kind=kOutput, calls=%fused_computation.28 | convolution fusion | flops 134217728 | bytes 4718592 | tf_op jit(solution)/shard_map/qik,qkn->qin/dot_general | solution.py:13
  43.2 24.3 %all-to-all-done = bf16[32,64,256]{2,1,0:T(8,128)(2,1)} async-done(((bf16[32,64,256]{2,1,0:T(8,128)(2,1)}), bf16[32,64,256]{2,1,0:T(8,128)(2,1)}, u32[]{:S(2)}, u32[]{:S(2)}) %all-to-all-start) | async-done | bytes 1048608 | tf_op jit(solution)/shard_map/all_to_all | solution.py:32
  67.5 1.4 convert_reduce_fusion.2
  69.2 17.4 %all-gather.1 = bf16[1024,256]{1,0:T(8,128)(2,1)S(1)} all-gather(bf16[64,256]{1,0:T(8,128)(2,1)S(1)} %get-tuple-element.36), channel_id=3, replica_groups=mesh['row'=16,'col'=32] {'row'}, dimensions={0}, use_global_device_ids=true | all-gather | bytes 557056 | tf_op jit(solution)/shard_map/all_gather | solution.py:45
  86.6 0.7 gather_fusion.2
  87.6 1.2 copy-done.2
  88.9 2.6 %fusion.1 = bf16[32,64,256]{2,1,0:T(8,128)(2,1)} fusion(f32[32,256,64]{1,2,0:T(8,128)S(1)} %copy-done.2, bf16[32,128,256]{2,1,0:T(8,128)(2,1)S(1)} %bitcast.164, bf16[6,1,1,32,64,128]{5,4,3,2,1,0:T(8,128)(2,1)} %param.8), kind=kOutput, calls=%fused_computation.19 | convolution fusion | flops 135266304 | bytes 5767168 | tf_op jit(solution)/shard_map/qik,qkn->qin/dot_general | solution.py:13
  91.5 5.2 %all-to-all-start.1 = ((bf16[32,64,256]{2,1,0:T(8,128)(2,1)}), bf16[32,64,256]{2,1,0:T(8,128)(2,1)}, u32[]{:S(2)}, u32[]{:S(2)}) async-start(bf16[32,64,256]{2,1,0:T(8,128)(2,1)} %fusion.1), calls=%async_computation.1 | async-start | bytes 2097152 | tf_op jit(solution)/shard_map/all_to_all | solution.py:32
  96.8 0.7 reshape.172
  98.6 0.7 copy.36
  99.5 0.7 gather_fusion.3
  100.2 0.7 copy.34
  100.9 0.8 copy.33
  103.3 2.8 %fusion.6 = f32[32,256,64]{1,2,0:T(8,128)} fusion(bf16[32,128,256]{2,1,0:T(8,128)(2,1)S(1)} %bitcast.161, bf16[6,1,1,32,64,128]{5,4,3,2,1,0:T(8,128)(2,1)} %param.8), kind=kOutput, calls=%fused_computation.25 | convolution fusion | flops 134217728 | bytes 4718592 | tf_op jit(solution)/shard_map/qik,qkn->qin/dot_general | solution.py:13
  106.1 0.7 gather_fusion.4
  107.1 2.8 %fusion.4 = f32[32,256,64]{1,2,0:T(8,128)} fusion(bf16[32,128,256]{2,1,0:T(8,128)(2,1)S(1)} %bitcast.162, bf16[6,1,1,32,64,128]{5,4,3,2,1,0:T(8,128)(2,1)} %param.8), kind=kOutput, calls=%fused_computation.23 | convolution fusion | flops 134217728 | bytes 4718592 | tf_op jit(solution)/shard_map/qik,qkn->qin/dot_general | solution.py:13
  110.0 15.9 %all-to-all-done.1 = bf16[32,64,256]{2,1,0:T(8,128)(2,1)} async-done(((bf16[32,64,256]{2,1,0:T(8,128)(2,1)}), bf16[32,64,256]{2,1,0:T(8,128)(2,1)}, u32[]{:S(2)}, u32[]{:S(2)}) %all-to-all-start.1) | async-done | bytes 1048608 | tf_op jit(solution)/shard_map/all_to_all | solution.py:32
  125.8 1.4 convert_reduce_fusion.1
  127.4 16.4 %all-gather.2 = bf16[1024,256]{1,0:T(8,128)(2,1)S(1)} all-gather(bf16[64,256]{1,0:T(8,128)(2,1)S(1)} %get-tuple-element.38), channel_id=4, replica_groups=mesh['row'=16,'col'=32] {'row'}, dimensions={0}, use_global_device_ids=true | all-gather | bytes 557056 | tf_op jit(solution)/shard_map/all_gather | solution.py:45
  143.8 0.7 gather_fusion.5
  144.8 1.2 copy-done
  146.7 1.7 fusion.2
  148.4 34.0 %all_to_all.15 = bf16[32,64,256]{2,1,0:T(8,128)(2,1)S(1)} all-to-all(bf16[32,64,256]{2,1,0:T(8,128)(2,1)S(1)} %fusion.2), channel_id=1, replica_groups=mesh['row'=16,'col'=32] {'col'}, dimensions={0} | all-to-all | bytes 2097152 | tf_op jit(solution)/shard_map/all_to_all | solution.py:32
  182.8 0.7 maximum_bitcast_fusion
  (58 shorter events, 7.2 us)
Async XLA Ops:
  28.9 38.6 %all-to-all-start = ((bf16[32,64,256]{2,1,0:T(8,128)(2,1)}), bf16[32,64,256]{2,1,0:T(8,128)(2,1)}, u32[]{:S(2)}, u32[]{:S(2)}) async-start(bf16[32,64,256]{2,1,0:T(8,128)(2,1)} %fusion), calls=%async_computation | async-start | bytes 2097152 | tf_op jit(solution)/shard_map/all_to_all | solution.py:32
  40.3 28.6 %copy-start.3 = (f32[4,1,1,64,64]{4,3,2,1,0:T(8,128)S(1)}, f32[4,1,1,64,64]{4,3,2,1,0:T(8,128)}, u32[]{:S(2)}) copy-start(f32[4,1,1,64,64]{4,3,2,1,0:T(8,128)} %param.7) | copy-start | bytes 196612
  40.3 28.6 %copy-start.4 = (bf16[4,1,1,64,256]{4,3,2,1,0:T(8,128)(2,1)S(1)}, bf16[4,1,1,64,256]{4,3,2,1,0:T(8,128)(2,1)}, u32[]{:S(2)}) copy-start(bf16[4,1,1,64,256]{4,3,2,1,0:T(8,128)(2,1)} %param.6) | copy-start | bytes 393220
  87.3 1.6 copy-start.2
  91.5 5.3 %copy-start.7 = (s32[32,2]{0,1:T(2,128)S(1)}, s32[32,2]{0,1:T(2,128)}, u32[]{:S(2)}) copy-start(s32[32,2]{0,1:T(2,128)} %get-tuple-element.33) | copy-start | bytes 772
  91.5 6.1 %copy-start.9 = (pred[32,2]{0,1:T(4,128)(4,1)S(1)}, pred[32,2]{0,1:T(4,128)(4,1)}, u32[]{:S(2)}) copy-start(pred[32,2]{0,1:T(4,128)(4,1)} %get-tuple-element.32) | copy-start | bytes 196
  91.5 6.2 %copy-start.11 = (pred[32,2]{0,1:T(4,128)(4,1)S(1)}, pred[32,2]{0,1:T(4,128)(4,1)}, u32[]{:S(2)}) copy-start(pred[32,2]{0,1:T(4,128)(4,1)} %get-tuple-element.23) | copy-start | bytes 196
  91.5 7.0 %copy-start.8 = (pred[32,2]{0,1:T(4,128)(4,1)S(1)}, pred[32,2]{0,1:T(4,128)(4,1)}, u32[]{:S(2)}) copy-start(pred[32,2]{0,1:T(4,128)(4,1)} %get-tuple-element.6) | copy-start | bytes 196
  91.5 7.1 %copy-start.10 = (pred[32,2]{0,1:T(4,128)(4,1)S(1)}, pred[32,2]{0,1:T(4,128)(4,1)}, u32[]{:S(2)}) copy-start(pred[32,2]{0,1:T(4,128)(4,1)} %get-tuple-element.18) | copy-start | bytes 196
  91.5 7.8 %copy-start.6 = (s32[32,2]{0,1:T(2,128)S(1)}, s32[32,2]{0,1:T(2,128)}, u32[]{:S(2)}) copy-start(s32[32,2]{0,1:T(2,128)} %get-tuple-element.31) | copy-start | bytes 772
  91.5 34.3 %all-to-all-start.1 = ((bf16[32,64,256]{2,1,0:T(8,128)(2,1)}), bf16[32,64,256]{2,1,0:T(8,128)(2,1)}, u32[]{:S(2)}, u32[]{:S(2)}) async-start(bf16[32,64,256]{2,1,0:T(8,128)(2,1)} %fusion.1), calls=%async_computation.1 | async-start | bytes 2097152 | tf_op jit(solution)/shard_map/all_to_all | solution.py:32
  106.1 0.7 copy-start.5
  144.5 1.6 copy-start
  144.5 2.2 %copy-start.1 = (f32[32,256,64]{1,2,0:T(8,128)S(1)}, f32[32,256,64]{1,2,0:T(8,128)}, u32[]{:S(2)}) copy-start(f32[32,256,64]{1,2,0:T(8,128)} %fusion.4) | copy-start | bytes 6291460
where the time goes:
time: 184 us; the launch traced here: 183 us
  blocking collectives  89.2 us (48%)
  waiting for transfers between devices  40.2 us (22%)
  matrix products  16.8 us (9%)
  starting transfers between devices  14.7 us (8%)
  local copies, waits for them, and re-layouts  12.6 us (7%)
  other arithmetic  9.61 us (5%)
    all_gather x3, blocking collectives, on_device(): gathered.append(lax.all_gather(solved[None], 'row', axis=0, tiled=True))  55.2 us
    all_to_all x2, waiting for transfers between devices, on_device(): lax.all_to_all(partial.astype(jnp.bfloat16), 'col', split_axis=0, concat_...  40.2 us
    all_to_all x1, blocking collectives, on_device(): lax.all_to_all(partial.astype(jnp.bfloat16), 'col', split_axis=0, concat_...  34 us
    dot_general x6, matrix products, level_terms(): jnp.einsum('qik,qkn->qin', blocks, picked, preferred_element_type=jnp.flo...  15.3 us
    all_to_all x2, starting transfers between devices, on_device(): lax.all_to_all(partial.astype(jnp.bfloat16), 'col', split_axis=0, concat_...  14.7 us
    gather x6, local copies, waits for them, and re-layouts, level_terms(): picked = jnp.take(gathered, clipped, axis=0)  4.08 us
  transfers between devices with their start and end apart: 2, of which 2 were waited for; matrix products, arithmetic and copies ran while one was open for 10% of the time, Pallas kernels for 0%

commit v1 on v0

--- a/solution.py
+++ b/solution.py
@@ -42,7 +42,16 @@
         results.append(solution)
         if section + 1 < levels:
             solved = solution.astype(jnp.bfloat16)
-            gathered.append(lax.all_gather(solved[None], "row", axis=0, tiled=True))
+            test_row = lambda group_axis, array_dim, point: jnp.concatenate(
+                lax.all_to_all(
+                    jnp.stack([point for _ in range(lax.axis_size(group_axis))]),
+                    axis_name=group_axis,
+                    concat_axis=0,
+                    split_axis=0,
+                ),
+                axis=array_dim,
+            )
+            gathered.append(test_row("row", 0, solved[None]))
     return jnp.stack(results)[:, None, None]
 
 

time: 184 us -> 198 us (1.076)
  the two profiles are of different devices: /device:TPU:8 before, /device:TPU:1 now
where the time goes in v1:
time: 198 us; the launch traced here: 196 us
  blocking collectives  72.2 us (36%)
  waiting for transfers between devices  61.6 us (31%)
  starting transfers between devices  23.4 us (12%)
  matrix products  17.9 us (9%)
  local copies, waits for them, and re-layouts  13.5 us (7%)
  other arithmetic  7.53 us (4%)
    all_to_all x2, blocking collectives, on_device(): lax.all_to_all(partial.astype(jnp.bfloat16), 'col', split_axis=0, concat_...  72.2 us
    all_to_all x3, waiting for transfers between devices, on_device(): lax.all_to_all(jnp.stack([point for _ in range(lax.axis_size(group_axis))...  38.7 us
    all_to_all x1, waiting for transfers between devices, on_device(): lax.all_to_all(partial.astype(jnp.bfloat16), 'col', split_axis=0, concat_...  22.9 us
    all_to_all x3, starting transfers between devices, on_device(): lax.all_to_all(jnp.stack([point for _ in range(lax.axis_size(group_axis))...  18.2 us
    dot_general x6, matrix products, level_terms(): jnp.einsum('qik,qkn->qin', blocks, picked, preferred_element_type=jnp.flo...  14.1 us
    gather x6, local copies, waits for them, and re-layouts, level_terms(): picked = jnp.take(gathered, clipped, axis=0)  5.43 us
    all_to_all x1, starting transfers between devices, on_device(): lax.all_to_all(partial.astype(jnp.bfloat16), 'col', split_axis=0, concat_...  5.25 us
  transfers between devices with their start and end apart: 4, of which 4 were waited for; matrix products, arithmetic and copies ran while one was open for 9% of the time, Pallas kernels for 0%

profile of v1, /device:TPU:1, one launch (start us, length us, event | category | flops | bytes accessed | tf_op | source)
XLA Modules:
  0.0 196.5 jit_solution(6789165908850378322)
XLA Ops:
  0.0 0.9 fusion.40
  0.9 0.9 stack.25
  1.8 10.2 %all-to-all-start = ((bf16[16,1,64,256]{3,2,1,0:T(8,128)(2,1)}), bf16[16,1,64,256]{3,2,1,0:T(8,128)(2,1)S(1)}, u32[]{:S(2)}, u32[]{:S(2)}) async-start(bf16[16,1,64,256]{3,2,1,0:T(8,128)(2,1)} %stack.25), calls=%async_computation | async-start | bytes 1048576 | tf_op jit(solution)/shard_map/all_to_all | solution.py:46
  12.0 0.8 compare_and_fusion.1
  13.1 0.8 compare_bitcast_fusion.1
  14.0 15.4 %all-to-all-done = bf16[16,1,64,256]{3,2,1,0:T(8,128)(2,1)S(1)} async-done(((bf16[16,1,64,256]{3,2,1,0:T(8,128)(2,1)}), bf16[16,1,64,256]{3,2,1,0:T(8,128)(2,1)S(1)}, u32[]{:S(2)}, u32[]{:S(2)}) %all-to-all-start) | async-done | bytes 524320 | tf_op jit(solution)/shard_map/all_to_all | solution.py:46
  30.4 1.5 fusion
  31.9 39.3 %all_to_all.30 = bf16[32,64,256]{2,1,0:T(8,128)(2,1)S(1)} all-to-all(bf16[32,64,256]{2,1,0:T(8,128)(2,1)S(1)} %fusion), channel_id=1, replica_groups=mesh['row'=16,'col'=32] {'col'}, dimensions={0} | all-to-all | bytes 2097152 | tf_op jit(solution)/shard_map/all_to_all | solution.py:32
  71.3 1.0 bitcast_convert_fusion.1
  72.3 0.9 stack.27
  73.2 4.0 %all-to-all-start.2 = ((bf16[16,1,64,256]{3,2,1,0:T(8,128)(2,1)}), bf16[16,1,64,256]{3,2,1,0:T(8,128)(2,1)S(1)}, u32[]{:S(2)}, u32[]{:S(2)}) async-start(bf16[16,1,64,256]{3,2,1,0:T(8,128)(2,1)} %stack.27), calls=%async_computation.2 | async-start | bytes 1048576 | tf_op jit(solution)/shard_map/all_to_all | solution.py:46
  78.0 0.7 gather_fusion.1
  79.0 2.8 %fusion.9 = f32[32,256,64]{1,2,0:T(8,128)} fusion(bf16[32,128,256]{2,1,0:T(8,128)(2,1)S(1)} %bitcast.160, bf16[6,1,1,32,64,128]{5,4,3,2,1,0:T(8,128)(2,1)} %param.8), kind=kOutput, calls=%fused_computation.28 | convolution fusion | flops 134217728 | bytes 4718592 | tf_op jit(solution)/shard_map/qik,qkn->qin/dot_general | solution.py:13
  81.8 12.6 %all-to-all-done.2 = bf16[16,1,64,256]{3,2,1,0:T(8,128)(2,1)S(1)} async-done(((bf16[16,1,64,256]{3,2,1,0:T(8,128)(2,1)}), bf16[16,1,64,256]{3,2,1,0:T(8,128)(2,1)S(1)}, u32[]{:S(2)}, u32[]{:S(2)}) %all-to-all-start.2) | async-done | bytes 524320 | tf_op jit(solution)/shard_map/all_to_all | solution.py:46
  95.5 1.2 copy-done.2
  96.7 2.6 %fusion.1 = bf16[32,64,256]{2,1,0:T(8,128)(2,1)} fusion(f32[32,256,64]{1,2,0:T(8,128)S(1)} %copy-done.2, bf16[32,128,256]{2,1,0:T(8,128)(2,1)S(1)} %bitcast.164, bf16[6,1,1,32,64,128]{5,4,3,2,1,0:T(8,128)(2,1)} %param.8), kind=kOutput, calls=%fused_computation.19 | convolution fusion | flops 135266304 | bytes 5767168 | tf_op jit(solution)/shard_map/qik,qkn->qin/dot_general | solution.py:13
  99.3 5.2 %all-to-all-start.3 = ((bf16[32,64,256]{2,1,0:T(8,128)(2,1)}), bf16[32,64,256]{2,1,0:T(8,128)(2,1)}, u32[]{:S(2)}, u32[]{:S(2)}) async-start(bf16[32,64,256]{2,1,0:T(8,128)(2,1)} %fusion.1), calls=%async_computation.3 | async-start | bytes 2097152 | tf_op jit(solution)/shard_map/all_to_all | solution.py:32
  105.8 2.0 %gather_fusion.3 = bf16[64,64,256]{2,1,0:T(8,128)(2,1)} fusion(bf16[16,64,256]{2,1,0:T(8,128)(2,1)S(1)} %bitcast.149, s32[1024]{0:T(1024)S(1)} %pad_clamp_fusion.2), kind=kCustom, calls=%fused_computation.3.clone | custom fusion | bytes 4194560 | tf_op jit(solution)/shard_map/jit(_take)/gather | solution.py:9
  107.8 1.9 select_select_fusion.2
  109.7 22.9 %all-to-all-done.3 = bf16[32,64,256]{2,1,0:T(8,128)(2,1)} async-done(((bf16[32,64,256]{2,1,0:T(8,128)(2,1)}), bf16[32,64,256]{2,1,0:T(8,128)(2,1)}, u32[]{:S(2)}, u32[]{:S(2)}) %all-to-all-start.3) | async-done | bytes 1048608 | tf_op jit(solution)/shard_map/all_to_all | solution.py:32
  132.6 1.4 convert_reduce_fusion.1
  134.0 1.0 bitcast_convert_fusion
  135.0 0.9 stack.29
  135.8 4.0 %all-to-all-start.4 = ((bf16[16,1,64,256]{3,2,1,0:T(8,128)(2,1)}), bf16[16,1,64,256]{3,2,1,0:T(8,128)(2,1)S(1)}, u32[]{:S(2)}, u32[]{:S(2)}) async-start(bf16[16,1,64,256]{3,2,1,0:T(8,128)(2,1)} %stack.29), calls=%async_computation.4 | async-start | bytes 1048576 | tf_op jit(solution)/shard_map/all_to_all | solution.py:46
  139.8 2.8 %fusion.6 = f32[32,256,64]{1,2,0:T(8,128)} fusion(bf16[32,128,256]{2,1,0:T(8,128)(2,1)S(1)} %bitcast.154, bf16[6,1,1,32,64,128]{5,4,3,2,1,0:T(8,128)(2,1)} %param.8), kind=kOutput, calls=%fused_computation.25 | convolution fusion | flops 134217728 | bytes 4718592 | tf_op jit(solution)/shard_map/qik,qkn->qin/dot_general | solution.py:13
  143.6 2.8 %fusion.4 = f32[32,256,64]{1,2,0:T(8,128)} fusion(bf16[32,128,256]{2,1,0:T(8,128)(2,1)S(1)} %bitcast.162, bf16[6,1,1,32,64,128]{5,4,3,2,1,0:T(8,128)(2,1)} %param.8), kind=kOutput, calls=%fused_computation.23 | convolution fusion | flops 134217728 | bytes 4718592 | tf_op jit(solution)/shard_map/qik,qkn->qin/dot_general | solution.py:13
  146.4 10.7 %all-to-all-done.4 = bf16[16,1,64,256]{3,2,1,0:T(8,128)(2,1)S(1)} async-done(((bf16[16,1,64,256]{3,2,1,0:T(8,128)(2,1)}), bf16[16,1,64,256]{3,2,1,0:T(8,128)(2,1)S(1)}, u32[]{:S(2)}, u32[]{:S(2)}) %all-to-all-start.4) | async-done | bytes 524320 | tf_op jit(solution)/shard_map/all_to_all | solution.py:46
  158.2 1.2 copy-done
  160.0 1.6 fusion.2
  161.7 33.0 %all_to_all.31 = bf16[32,64,256]{2,1,0:T(8,128)(2,1)S(1)} all-to-all(bf16[32,64,256]{2,1,0:T(8,128)(2,1)S(1)} %fusion.2), channel_id=1, replica_groups=mesh['row'=16,'col'=32] {'col'}, dimensions={0} | all-to-all | bytes 2097152 | tf_op jit(solution)/shard_map/all_to_all | solution.py:32
  194.8 1.0 convolution_bitcast_fusion
  195.8 0.7 maximum_bitcast_fusion
  (47 shorter events, 7.7 us)
Async XLA Ops:
  1.8 27.6 %all-to-all-start = ((bf16[16,1,64,256]{3,2,1,0:T(8,128)(2,1)}), bf16[16,1,64,256]{3,2,1,0:T(8,128)(2,1)S(1)}, u32[]{:S(2)}, u32[]{:S(2)}) async-start(bf16[16,1,64,256]{3,2,1,0:T(8,128)(2,1)} %stack.25), calls=%async_computation | async-start | bytes 1048576 | tf_op jit(solution)/shard_map/all_to_all | solution.py:46
  31.9 39.4 %copy-start.3 = (f32[4,1,1,64,64]{4,3,2,1,0:T(8,128)S(1)}, f32[4,1,1,64,64]{4,3,2,1,0:T(8,128)}, u32[]{:S(2)}) copy-start(f32[4,1,1,64,64]{4,3,2,1,0:T(8,128)} %param.7) | copy-start | bytes 196612
  73.2 21.3 %all-to-all-start.2 = ((bf16[16,1,64,256]{3,2,1,0:T(8,128)(2,1)}), bf16[16,1,64,256]{3,2,1,0:T(8,128)(2,1)S(1)}, u32[]{:S(2)}, u32[]{:S(2)}) async-start(bf16[16,1,64,256]{3,2,1,0:T(8,128)(2,1)} %stack.27), calls=%async_computation.2 | async-start | bytes 1048576 | tf_op jit(solution)/shard_map/all_to_all | solution.py:46
  95.1 1.6 copy-start.2
  99.3 33.3 %all-to-all-start.3 = ((bf16[32,64,256]{2,1,0:T(8,128)(2,1)}), bf16[32,64,256]{2,1,0:T(8,128)(2,1)}, u32[]{:S(2)}, u32[]{:S(2)}) async-start(bf16[32,64,256]{2,1,0:T(8,128)(2,1)} %fusion.1), calls=%async_computation.3 | async-start | bytes 2097152 | tf_op jit(solution)/shard_map/all_to_all | solution.py:32
  135.8 21.3 %all-to-all-start.4 = ((bf16[16,1,64,256]{3,2,1,0:T(8,128)(2,1)}), bf16[16,1,64,256]{3,2,1,0:T(8,128)(2,1)S(1)}, u32[]{:S(2)}, u32[]{:S(2)}) async-start(bf16[16,1,64,256]{3,2,1,0:T(8,128)(2,1)} %stack.29), calls=%async_computation.4 | async-start | bytes 1048576 | tf_op jit(solution)/shard_map/all_to_all | solution.py:46
  157.8 1.6 copy-start
  157.8 2.2 %copy-start.1 = (f32[32,256,64]{1,2,0:T(8,128)S(1)}, f32[32,256,64]{1,2,0:T(8,128)}, u32[]{:S(2)}) copy-start(f32[32,256,64]{1,2,0:T(8,128)} %fusion.4) | copy-start | bytes 6291460
